TPU v7x, 512 devices: a whole 4x4x16 slice. The times are simulated.
512 devices in a mesh: fsdp: 8 (over y, x_lo), tensor: 64 (over x_hi, z, core).
Axes of the slice: x: 4 (x_hi: 2, x_lo: 2; x = x_hi * 2 + x_lo), y: 4, z: 16, core: 2. Of those that a mesh axis runs over, the one named last changes fastest.
Arguments:
- tokens: bfloat16 [1024, 8192], P('fsdp', 'tensor'), may hold values from -6 to 6
- in_values: bfloat16 [8192, 3, 8192], P('fsdp', None, 'tensor'), may hold values from -0.1875 to 0.1875
- in_scales: bfloat16 [64, 3, 8192], P('fsdp', None, 'tensor'), may hold values from 0.5 to 2
- filters: float32 [512, 128], P('tensor'), may hold values from -0.6 to 0.6
- out_weight: bfloat16 [8192, 8192], P('tensor', 'fsdp'), may hold values from -0.0625 to 0.0625
- cotangent: bfloat16 [1024, 8192], P('fsdp', 'tensor'), may hold values from -15 to 15
Outputs:
- input_grad: bfloat16 [1024, 8192], P('fsdp', 'tensor')
- filter_grad: float32 [512, 128], P('tensor')
All inputs are finite; a program needn't handle non-finite values.
Results may differ from a plain program's by a relative error of at most 0.012.
Values may be sent and summed in bfloat16 or wider, within the bound.
A program may use at most 128 MiB of HBM per device.

v0:
```python
import jax
import jax.numpy as jnp
from jax import lax
from jax.sharding import PartitionSpec as P

BLOCK = 128


def passed_along(array, axis, by):
    length = lax.axis_size(axis)
    pairs = [(i, i + by) for i in range(length) if 0 <= i + by < length]
    return lax.ppermute(array, axis, pairs)


def dequantize(values, scales):
    blocks = scales.shape[0]
    channels = values.shape[2]
    scaled = (
        values.astype(jnp.float32).reshape(blocks, BLOCK, 3, channels)
        * scales.astype(jnp.float32)[:, None]
    )
    return scaled.reshape(blocks * BLOCK, 3 * channels).astype(jnp.bfloat16)


def apply_taps(filt, extended, rows, per_group, causal):
    taps = filt.shape[1]
    repeated = jnp.repeat(filt, per_group, axis=0)

    def one_step(lag_index, total):
        lag_value = jnp.asarray(lag_index).astype(jnp.int32)
        offset = taps - 1 - lag_value if causal else lag_value
        slab = lax.dynamic_slice_in_dim(extended, offset, rows, 0)
        column = lax.dynamic_slice_in_dim(repeated, lag_value, 1, 1)[:, 0]
        return total + column[None, :] * slab

    return lax.fori_loop(0, taps, one_step, jnp.zeros((rows, repeated.shape[0]), jnp.float32))


def filter_terms(grad_rows, extended, groups_here, per_group, taps):
    rows = grad_rows.shape[0]
    ext_rows = extended.shape[0]
    corr = jnp.einsum(
        "tgj,ugj->gtu",
        grad_rows.reshape(rows, groups_here, per_group),
        extended.reshape(ext_rows, groups_here, per_group),
        precision=lax.Precision.HIGHEST,
    )
    flat = jnp.concatenate(
        [corr.reshape(groups_here, rows * ext_rows), jnp.zeros((groups_here, rows), jnp.float32)], 1
    )
    diagonal = flat.reshape(groups_here, rows, ext_rows + 1)[:, :, :taps]
    return jnp.sum(diagonal, axis=1)[:, ::-1]


def fetch_out(out_weight):
    return lax.all_gather(out_weight, "fsdp", axis=1, tiled=True)


def on_device(tokens, in_values, in_scales, filters, out_weight, cotangent):
    rows = tokens.shape[0]
    channels = tokens.shape[1]
    groups_here, taps = filters.shape
    per_group = channels // groups_here
    whole = lax.all_gather(tokens, "tensor", axis=1, tiled=True)
    values, scales = (
        lax.all_gather(in_values, "fsdp", axis=0, tiled=True),
        lax.all_gather(in_scales, "fsdp", axis=0, tiled=True),
    )
    weight = dequantize(values, scales)
    proj = (
        jnp.dot(whole, weight, preferred_element_type=jnp.float32)
        .astype(jnp.bfloat16)
        .reshape(rows, 3, channels)
    )
    query = proj[:, 0].astype(jnp.float32)
    key_part = proj[:, 1].astype(jnp.float32)
    value_part = proj[:, 2].astype(jnp.float32)
    product = key_part * value_part
    earlier = passed_along(product[rows - (taps - 1) :].astype(jnp.bfloat16), "fsdp", 1).astype(
        jnp.float32
    )
    extended = jnp.concatenate([earlier, product], 0)
    conv = apply_taps(filters, extended, rows, per_group, True)
    out_full = fetch_out(out_weight)
    cot_whole = lax.all_gather(cotangent, "tensor", axis=1, tiled=True)
    grad_z = lax.dot_general(
        cot_whole, out_full, (((1,), (1,)), ((), ())), preferred_element_type=jnp.float32
    )
    grad_query = grad_z * conv
    grad_conv = grad_z * query
    following = passed_along(grad_conv[: taps - 1].astype(jnp.bfloat16), "fsdp", -1).astype(
        jnp.float32
    )
    grad_ext = jnp.concatenate([grad_conv, following], 0)
    grad_product = apply_taps(filters, grad_ext, rows, per_group, False)
    grad_proj = jnp.stack([grad_query, grad_product * value_part, grad_product * key_part], axis=1)
    grad_proj = grad_proj.astype(jnp.bfloat16).reshape(rows, 3 * channels)
    summed = lax.psum_scatter(
        lax.dot_general(
            weight, grad_proj, (((1,), (1,)), ((), ())), preferred_element_type=jnp.float32
        ),
        "tensor",
        scatter_dimension=0,
        tiled=True,
    )
    input_grad = summed.T.astype(jnp.bfloat16)
    local_filter = filter_terms(grad_conv, extended, groups_here, per_group, taps) / rows
    filter_grad = lax.psum(local_filter, "fsdp")
    return (input_grad, filter_grad)


def solution(mesh):
    placed = (
        P("fsdp", "tensor"),
        P("fsdp", None, "tensor"),
        P("fsdp", None, "tensor"),
        P("tensor", None),
        P("tensor", "fsdp"),
        P("fsdp", "tensor"),
    )
    return jax.shard_map(
        on_device,
        mesh=mesh,
        in_specs=placed,
        out_specs=(P("fsdp", "tensor"), P("tensor", None)),
        check_vma=False,
    )
```

profile of v0, /device:TPU:8, one launch (start us, length us, event | category | flops | bytes accessed | tf_op | source)
XLA Modules:
  0.0 812.5 jit_solution(18194216193005715439)
XLA Ops:
  7.2 2.3 copy.16
  9.6 0.7 all-gather.11.cloned.1.call-update
  10.3 0.7 all-gather.9.cloned.1.call-update
  11.1 0.5 all-gather.7.cloned.1.call-update
  11.7 29.2 %all_gather.16 = bf16[64,3,128]{2,0,1:T(8,128)(2,1)S(1)} all-gather(bf16[8,3,128]{2,0,1:T(8,128)(2,1)} %param.12), channel_id=1, replica_groups=mesh['fsdp'=8,'tensor'=64] {'fsdp'}, dimensions={0}, use_global_device_ids=true | all-gather | bytes 55296 | tf_op jit(solution)/shard_map/all_gather | solution.py:67
  40.8 0.1 copy.17
  41.0 110.4 %all-gather.5.cloned.1.call-done = bf16[8192,3,128]{0,2,1:T(8,128)(2,1)} async-done(((bf16[1024,3,128]{0,2,1:T(8,128)(2,1)}), bf16[8192,3,128]{0,2,1:T(8,128)(2,1)}) %all-gather.5.cloned.1.call-update) | async-done | bytes 6291472 | tf_op jit(solution)/shard_map/all_gather | solution.py:66
  151.4 7.2 mul.88
  158.6 16.8 %fusion = bf16[8192,384]{0,1:T(8,128)(2,1)} fusion(f32[48,8,64,128]{3,2,1,0:T(8,128)} %bitcast.64, bf16[8192,3,128]{0,2,1:T(8,128)(2,1)} %all-gather.5.cloned.1.call-done), kind=kLoop, calls=%fused_computation.7 | loop fusion | flops 9437184 | bytes 25165824 | tf_op jit(solution)/shard_map/convert_element_type | solution.py:22
  175.3 117.4 %all-gather.11.cloned.1.call-done = bf16[128,8192]{1,0:T(8,128)(2,1)} async-done(((bf16[128,128]{1,0:T(8,128)(2,1)}), bf16[128,8192]{1,0:T(8,128)(2,1)}) %all-gather.11.cloned.1.call-update) | async-done | bytes 2097168 | tf_op jit(solution)/shard_map/all_gather | solution.py:64
  292.7 5.2 convolution_convert_fusion
  297.9 49.0 %all-gather.9.cloned.1.call-done = bf16[128,8192]{1,0:T(8,128)(2,1)} async-done(((bf16[128,1024]{1,0:T(8,128)(2,1)}), bf16[128,8192]{1,0:T(8,128)(2,1)}) %all-gather.9.cloned.1.call-update) | async-done | bytes 2097168 | tf_op jit(solution)/shard_map/all_gather | solution.py:56
  347.0 141.2 %all-gather.7.cloned.1.call-done = bf16[128,8192]{1,0:T(8,128)(2,1)} async-done(((bf16[128,128]{1,0:T(8,128)(2,1)}), bf16[128,8192]{1,0:T(8,128)(2,1)}) %all-gather.7.cloned.1.call-update) | async-done | bytes 2097168 | tf_op jit(solution)/shard_map/all_gather | solution.py:85
  488.2 2.9 convert_multiply_fusion.1
  491.2 2.7 collective-permute-start
  493.9 13.8 %mul.89 = f32[8192,3,128]{0,2,1:T(8,128)} reshape(f32[64,128,3,128]{1,0,3,2:T(8,128)} %mul.88) | data formatting | bytes 25165824 | tf_op jit(solution)/shard_map/mul | solution.py:19
  507.8 4.3 collective-permute-start.1
  512.1 0.1 pad_maximum_fusion
  512.2 33.2 %while.30 = (s32[]{:T(128)}, f32[128,128]{1,0:T(8,128)S(1)}, f32[128,128]{0,1:T(8,128)S(1)}, f32[255,128]{0,1:T(8,128)S(1)}, s32[]{:T(128)}, /*index=5*/s32[]{:T(128)}, s32[]{:T(128)}, s32[]{:T(128)}) while((s32[]{:T(128)}, f32[128,128]{1,0:T(8,128)S(1)}, f32[128,128]{0,1:T(8,128)S(1)}, f32[255,128]{0,1:T(8,128)S(1)}, s32[]{:T(128)}, ...), condition=%wide.region_1.0_spmd.clone, body=%wide.region_0.0_spmd.clone.sunk | while | flops 49159 | bytes 460437 | solution.py:36
  512.3 0.1 copy.36
  513.1 0.1 copy.36
  513.9 0.1 copy.36
  514.7 0.1 copy.36
  545.6 32.5 %while.31 = (s32[]{:T(128)}, f32[128,128]{1,0:T(8,128)S(1)}, f32[128,128]{0,1:T(8,128)S(1)}, f32[255,128]{0,1:T(8,128)S(1)}, s32[]{:T(128)}, /*index=5*/s32[]{:T(128)}) while((s32[]{:T(128)}, f32[128,128]{1,0:T(8,128)S(1)}, f32[128,128]{0,1:T(8,128)S(1)}, f32[255,128]{0,1:T(8,128)S(1)}, s32[]{:T(128)}, /*index=5*/s32[]{:T(128)}) %tuple.96), condition=%wide.region_3.0_spmd.clone, body=%wide.region_2.0_spmd.clone.sunk | while | flops 49155 | bytes 460375 | solution.py:36
  578.3 10.5 %convolution_bitcast_fusion = f32[8192,128]{1,0:T(8,128)} fusion(f32[8192,3,128]{0,2,1:T(8,128)} %mul.89, bf16[8192,3,128]{0,2,1:T(8,128)(2,1)} %all-gather.5.cloned.1.call-done, bf16[128,1,128]{0,2,1:T(8,128)(2,1)S(1)} %get-tuple-element.260, bf16[128,1,128]{0,2,1:T(8,128)(2,1)S(1)} %get-tuple-element.259, bf16[128,1,128]{0,2,1:T(8,128)(2,1)S(1)} %fusion.9), kind=kOutput, calls=%fused_computation.9 | convolution fusion | flops 814841856 | bytes 23166976 | tf_op jit(solution)/shard_map/dot_general | solution.py:99
  588.8 1.0 fusion.13
  589.8 0.6 reshape.48
  590.5 0.1 slice_reduce_fusion
  590.7 16.3 %psum.7 = f32[8,128]{1,0:T(8,128)} all-reduce(f32[8,128]{1,0:T(8,128)S(1)} %broadcast_multiply_fusion), channel_id=1, replica_groups=mesh['fsdp'=8,'tensor'=64] {'fsdp'}, use_global_device_ids=true, to_apply=%region_6.0 | all-reduce | flops 1024 | bytes 8192 | tf_op jit(solution)/shard_map/psum | solution.py:108
  607.0 197.4 %reduce-scatter.2.cloned.1.call-done = f32[128,128]{1,0:T(8,128)} async-done(((f32[8192,128]{1,0:T(8,128)}), f32[128,128]{1,0:T(8,128)}) %reduce-scatter.2.cloned.1.call-update) | async-done | bytes 65552 | tf_op jit(solution)/shard_map/reduce_scatter | solution.py:98
  804.4 0.8 convert_bitcast_fusion
  805.2 0.7 copy.27
  (1047 shorter events, 53.5 us)
Async XLA Ops:
  7.2 144.2 %all-gather.5.cloned.1.call-start = ((), (), s32[]{:S(2)}) async-start(), calls=%async_computation.1 | async-start | bytes 7077888 | tf_op jit(solution)/shard_map/all_gather | solution.py:66
  9.5 283.2 %all-gather.11.cloned.1.call-start = ((), (), s32[]{:S(2)}) async-start(), calls=%async_computation.4 | async-start | bytes 2129920 | tf_op jit(solution)/shard_map/all_gather | solution.py:64
  10.3 336.7 %all-gather.9.cloned.1.call-start = ((), (), s32[]{:S(2)}) async-start(), calls=%async_computation.3 | async-start | bytes 2359296 | tf_op jit(solution)/shard_map/all_gather | solution.py:56
  11.0 477.2 %all-gather.7.cloned.1.call-start = ((), (), s32[]{:S(2)}) async-start(), calls=%async_computation.2 | async-start | bytes 2129920 | tf_op jit(solution)/shard_map/all_gather | solution.py:85
  11.6 792.8 %reduce-scatter.2.cloned.1.call-start = ((), (), s32[]{:S(2)}) async-start(), calls=%async_computation.5 | async-start | bytes 4259840 | tf_op jit(solution)/shard_map/reduce_scatter | solution.py:98
  491.2 20.9 %collective-permute-start = (bf16[127,128]{0,1:T(8,128)(2,1)S(1)}, bf16[127,128]{0,1:T(8,128)(2,1)S(1)}, u32[]{:S(2)}, u32[]{:S(2)}) collective-permute-start(bf16[127,128]{0,1:T(8,128)(2,1)S(1)} %slice.49), channel_id=1, source_target_pairs={{0,64},{64,128},{128,192},{192,256},{256,320},{320,384},{384,448},... | collective-permute-start | bytes 97544 | tf_op jit(solution)/shard_map/ppermute | solution.py:12
  493.9 13.8 %copy-start = (f32[8,128]{1,0:T(8,128)S(1)}, f32[8,128]{1,0:T(8,128)}, u32[]{:S(2)}) copy-start(f32[8,128]{1,0:T(8,128)} %param.13) | copy-start | bytes 12292
  507.8 37.7 %collective-permute-start.1 = (bf16[127,128]{0,1:T(8,128)(2,1)S(1)}, bf16[127,128]{0,1:T(8,128)(2,1)S(1)}, u32[]{:S(2)}, u32[]{:S(2)}) collective-permute-start(bf16[127,128]{0,1:T(8,128)(2,1)S(1)} %slice.48), channel_id=1, source_target_pairs={{64,0},{128,64},{192,128},{256,192},{320,256},{384,320},{448,384},... | collective-permute-start | bytes 97544 | tf_op jit(solution)/shard_map/ppermute | solution.py:12
Sparse Core Ops, SparseCore 0:
  10.1 141.2 all-gather.4
  154.4 138.2 all-gather.10
  294.8 52.1 all-gather.8
  349.8 138.3 all-gather.6
  588.9 215.4 reduce-scatter.1
where the time goes:
time: 813 us; the launch traced here: 812 us
  waiting for transfers between devices  617 us (76%)
  local copies, waits for them, and re-layouts  73.6 us (9%)
  blocking collectives  45.5 us (6%)
  other arithmetic  22.5 us (3%)
  matrix products  19.7 us (2%)
  between operations  14 us (2%)
  loops' own time  12.7 us (2%)
    reduce_scatter x1, waiting for transfers between devices, on_device(): lax.psum_scatter(lax.dot_general(weight, grad_proj, (((1,), (1,)), ((), (...  197 us
    all_gather x1, waiting for transfers between devices, on_device(): cot_whole = lax.all_gather(cotangent, 'tensor', axis=1, tiled=True)  141 us
    all_gather x1, waiting for transfers between devices, on_device(): whole = lax.all_gather(tokens, 'tensor', axis=1, tiled=True)  117 us
    all_gather x1, waiting for transfers between devices, on_device(): lax.all_gather(in_values, 'fsdp', axis=0, tiled=True)  110 us
    all_gather x1, waiting for transfers between devices, fetch_out(): return lax.all_gather(out_weight, 'fsdp', axis=1, tiled=True)  49 us
    dynamic_slice x512, local copies, waits for them, and re-layouts, one_step(): slab = lax.dynamic_slice_in_dim(extended, offset, rows, 0)  45.3 us
    all_gather x1, blocking collectives, on_device(): lax.all_gather(in_scales, 'fsdp', axis=0, tiled=True)  29.2 us
    mul x2, local copies, waits for them, and re-layouts, dequantize(): values.astype(jnp.float32).reshape(blocks, BLOCK, 3, channels)  21 us
  transfers between devices with their start and end apart: 7, of which 5 were waited for; matrix products, arithmetic and copies ran while one was open for 9% of the time, Pallas kernels for 0%

commit v1 on v0

--- a/solution.py
+++ b/solution.py
@@ -82,7 +82,9 @@
     extended = jnp.concatenate([earlier, product], 0)
     conv = apply_taps(filters, extended, rows, per_group, True)
     out_full = fetch_out(out_weight)
-    cot_whole = lax.all_gather(cotangent, "tensor", axis=1, tiled=True)
+    cot_whole = jnp.concatenate(
+        lax.all_to_all(jnp.stack([cotangent] * lax.axis_size("tensor")), "tensor", 0, 0), axis=1
+    )
     grad_z = lax.dot_general(
         cot_whole, out_full, (((1,), (1,)), ((), ())), preferred_element_type=jnp.float32
     )

time: 813 us -> 702 us (0.86)
  waiting for transfers between devices: 617 us -> 490 us
  starting transfers between devices: 7.11 us -> 25.6 us
    all_gather x1 -> x0, waiting for transfers between devices: 141 us -> none  [on_device(): cot_whole = lax.all_gather(cotangent, 'tensor', axis=1, tiled=True)]
    all_to_all x0 -> x1, starting transfers between devices: none -> 18.6 us  [on_device(): lax.all_to_all(jnp.stack([cotangent] * lax.axis_size('tensor')), 'tensor'...]
  transfers between devices with their start and end apart: 7 -> 7, of which waited for: 5 -> 4; matrix products, arithmetic and copies ran while one was open for 9% -> 11% of each run, Pallas kernels for 0% -> 0%
where the time goes in v1:
time: 702 us; the launch traced here: 701 us
  waiting for transfers between devices  490 us (70%)
  local copies, waits for them, and re-layouts  76.3 us (11%)
  blocking collectives  40.9 us (6%)
  starting transfers between devices  25.6 us (4%)
  other arithmetic  22.5 us (3%)
  matrix products  19 us (3%)
  between operations  14 us (2%)
  loops' own time  12.7 us (2%)
    reduce_scatter x1, waiting for transfers between devices, on_device(): lax.psum_scatter(lax.dot_general(weight, grad_proj, (((1,), (1,)), ((), (...  205 us
    all_gather x1, waiting for transfers between devices, on_device(): whole = lax.all_gather(tokens, 'tensor', axis=1, tiled=True)  118 us
    all_gather x1, waiting for transfers between devices, on_device(): lax.all_gather(in_values, 'fsdp', axis=0, tiled=True)  117 us
    all_gather x1, waiting for transfers between devices, fetch_out(): return lax.all_gather(out_weight, 'fsdp', axis=1, tiled=True)  49 us
    dynamic_slice x512, local copies, waits for them, and re-layouts, one_step(): slab = lax.dynamic_slice_in_dim(extended, offset, rows, 0)  45.3 us
    all_gather x1, blocking collectives, on_device(): lax.all_gather(in_scales, 'fsdp', axis=0, tiled=True)  24.6 us
    mul x2, local copies, waits for them, and re-layouts, dequantize(): values.astype(jnp.float32).reshape(blocks, BLOCK, 3, channels)  21 us
    all_to_all x1, starting transfers between devices, on_device(): lax.all_to_all(jnp.stack([cotangent] * lax.axis_size('tensor')), 'tensor'...  18.6 us
  transfers between devices with their start and end apart: 7, of which 4 were waited for; matrix products, arithmetic and copies ran while one was open for 11% of the time, Pallas kernels for 0%

profile of v1, /device:TPU:8, one launch (start us, length us, event | category | flops | bytes accessed | tf_op | source)
XLA Modules:
  0.0 701.5 jit_solution(14273591543560967045)
XLA Ops:
  7.2 2.3 copy.16
  9.6 0.9 copy.18
  10.4 1.8 stack.14
  12.2 18.6 %all-to-all-start = ((bf16[64,128,128]{1,2,0:T(8,128)(2,1)}), bf16[64,128,128]{1,2,0:T(8,128)(2,1)S(1)}, u32[]{:S(2)}, u32[]{:S(2)}) async-start(bf16[64,128,128]{1,2,0:T(8,128)(2,1)} %stack.14), calls=%async_computation | async-start | bytes 4194304 | tf_op jit(solution)/shard_map/all_to_all | solution.py:86
  30.9 0.7 all-gather.8.cloned.1.call-update
  31.6 0.7 all-gather.6.cloned.1.call-update
  32.4 24.6 %all_gather.13 = bf16[64,3,128]{2,0,1:T(8,128)(2,1)S(1)} all-gather(bf16[8,3,128]{2,0,1:T(8,128)(2,1)S(1)} %copy-done), channel_id=1, replica_groups=mesh['fsdp'=8,'tensor'=64] {'fsdp'}, dimensions={0}, use_global_device_ids=true | all-gather | bytes 55296 | tf_op jit(solution)/shard_map/all_gather | solution.py:67
  56.9 0.1 copy.17
  57.0 117.4 %all-gather.4.cloned.1.call-done = bf16[8192,3,128]{0,2,1:T(8,128)(2,1)} async-done(((bf16[1024,3,128]{0,2,1:T(8,128)(2,1)}), bf16[8192,3,128]{0,2,1:T(8,128)(2,1)}) %all-gather.4.cloned.1.call-update) | async-done | bytes 6291472 | tf_op jit(solution)/shard_map/all_gather | solution.py:66
  174.4 7.2 %mul.88 = f32[64,128,3,128]{1,0,3,2:T(8,128)} broadcast(f32[64,3,128]{0,2,1:T(8,128)S(1)} %copy.17), dimensions={0,2,3} | broadcast | bytes 12681216 | tf_op jit(solution)/shard_map/mul | solution.py:19
  181.6 16.8 %fusion = bf16[8192,384]{0,1:T(8,128)(2,1)} fusion(f32[48,8,64,128]{3,2,1,0:T(8,128)} %bitcast.67, bf16[8192,3,128]{0,2,1:T(8,128)(2,1)} %all-gather.4.cloned.1.call-done), kind=kLoop, calls=%fused_computation.7 | loop fusion | flops 9437184 | bytes 25165824 | tf_op jit(solution)/shard_map/convert_element_type | solution.py:22
  198.4 117.6 %all-gather.8.cloned.1.call-done = bf16[128,8192]{1,0:T(8,128)(2,1)} async-done(((bf16[128,128]{1,0:T(8,128)(2,1)}), bf16[128,8192]{1,0:T(8,128)(2,1)}) %all-gather.8.cloned.1.call-update) | async-done | bytes 2097168 | tf_op jit(solution)/shard_map/all_gather | solution.py:64
  316.0 5.2 convolution_convert_fusion
  321.2 49.0 %all-gather.6.cloned.1.call-done = bf16[128,8192]{1,0:T(8,128)(2,1)} async-done(((bf16[128,1024]{1,0:T(8,128)(2,1)}), bf16[128,8192]{1,0:T(8,128)(2,1)}) %all-gather.6.cloned.1.call-update) | async-done | bytes 2097168 | tf_op jit(solution)/shard_map/all_gather | solution.py:56
  370.2 2.3 convert_multiply_fusion.1
  372.6 3.4 collective-permute-start
  376.0 13.8 %mul.89 = f32[8192,3,128]{0,2,1:T(8,128)} reshape(f32[64,128,3,128]{1,0,3,2:T(8,128)} %mul.88) | data formatting | bytes 25165824 | tf_op jit(solution)/shard_map/mul | solution.py:19
  390.0 3.5 collective-permute-start.1
  393.5 0.1 pad_maximum_fusion
  393.6 33.2 %while.30 = (s32[]{:T(128)}, f32[128,128]{1,0:T(8,128)S(1)}, f32[128,128]{0,1:T(8,128)S(1)}, f32[255,128]{0,1:T(8,128)S(1)}, s32[]{:T(128)}, /*index=5*/s32[]{:T(128)}, s32[]{:T(128)}, s32[]{:T(128)}) while((s32[]{:T(128)}, f32[128,128]{1,0:T(8,128)S(1)}, f32[128,128]{0,1:T(8,128)S(1)}, f32[255,128]{0,1:T(8,128)S(1)}, s32[]{:T(128)}, ...), condition=%wide.region_1.0_spmd.clone, body=%wide.region_0.0_spmd.clone.sunk | while | flops 49159 | bytes 460437 | solution.py:36
  393.7 0.1 copy.37
  394.5 0.1 copy.37
  395.3 0.1 copy.37
  427.0 32.5 %while.31 = (s32[]{:T(128)}, f32[128,128]{1,0:T(8,128)S(1)}, f32[128,128]{0,1:T(8,128)S(1)}, f32[255,128]{0,1:T(8,128)S(1)}, s32[]{:T(128)}, /*index=5*/s32[]{:T(128)}) while((s32[]{:T(128)}, f32[128,128]{1,0:T(8,128)S(1)}, f32[128,128]{0,1:T(8,128)S(1)}, f32[255,128]{0,1:T(8,128)S(1)}, s32[]{:T(128)}, /*index=5*/s32[]{:T(128)}) %tuple.94), condition=%wide.region_3.0_spmd.clone, body=%wide.region_2.0_spmd.clone.sunk | while | flops 49155 | bytes 460375 | solution.py:36
  459.7 10.5 %convolution_bitcast_fusion = f32[8192,128]{1,0:T(8,128)} fusion(f32[8192,3,128]{0,2,1:T(8,128)} %mul.89, bf16[8192,3,128]{0,2,1:T(8,128)(2,1)} %all-gather.4.cloned.1.call-done, bf16[128,1,128]{0,2,1:T(8,128)(2,1)S(1)} %get-tuple-element.260, bf16[128,1,128]{0,2,1:T(8,128)(2,1)S(1)} %get-tuple-element.259, bf16[128,1,128]{0,2,1:T(8,128)(2,1)S(1)} %fusion.9), kind=kOutput, calls=%fused_computation.9 | convolution fusion | flops 814841856 | bytes 23166976 | tf_op jit(solution)/shard_map/dot_general | solution.py:101
  470.2 1.0 fusion.13
  471.2 0.6 reshape.58
  471.9 0.1 slice_reduce_fusion
  472.1 16.3 %psum.7 = f32[8,128]{1,0:T(8,128)} all-reduce(f32[8,128]{1,0:T(8,128)S(1)} %broadcast_multiply_fusion), channel_id=1, replica_groups=mesh['fsdp'=8,'tensor'=64] {'fsdp'}, use_global_device_ids=true, to_apply=%region_6.0 | all-reduce | flops 1024 | bytes 8192 | tf_op jit(solution)/shard_map/psum | solution.py:110
  488.5 204.9 %reduce-scatter.2.cloned.1.call-done = f32[128,128]{1,0:T(8,128)} async-done(((f32[8192,128]{1,0:T(8,128)}), f32[128,128]{1,0:T(8,128)}) %reduce-scatter.2.cloned.1.call-update) | async-done | bytes 65552 | tf_op jit(solution)/shard_map/reduce_scatter | solution.py:100
  693.4 0.8 convert_bitcast_fusion
  694.2 0.7 copy.28
  (1050 shorter events, 53.5 us)
Async XLA Ops:
  7.2 25.2 %copy-start = (bf16[8,3,128]{2,0,1:T(8,128)(2,1)S(1)}, bf16[8,3,128]{2,0,1:T(8,128)(2,1)}, u32[]{:S(2)}) copy-start(bf16[8,3,128]{2,0,1:T(8,128)(2,1)} %param.12) | copy-start | bytes 18436
  7.2 167.3 %all-gather.4.cloned.1.call-start = ((), (), s32[]{:S(2)}) async-start(), calls=%async_computation.2 | async-start | bytes 7077888 | tf_op jit(solution)/shard_map/all_gather | solution.py:66
  12.2 358.0 %all-to-all-start = ((bf16[64,128,128]{1,2,0:T(8,128)(2,1)}), bf16[64,128,128]{1,2,0:T(8,128)(2,1)S(1)}, u32[]{:S(2)}, u32[]{:S(2)}) async-start(bf16[64,128,128]{1,2,0:T(8,128)(2,1)} %stack.14), calls=%async_computation | async-start | bytes 4194304 | tf_op jit(solution)/shard_map/all_to_all | solution.py:86
  30.8 285.2 %all-gather.8.cloned.1.call-start = ((), (), s32[]{:S(2)}) async-start(), calls=%async_computation.4 | async-start | bytes 2129920 | tf_op jit(solution)/shard_map/all_gather | solution.py:64
  31.6 338.7 %all-gather.6.cloned.1.call-start = ((), (), s32[]{:S(2)}) async-start(), calls=%async_computation.3 | async-start | bytes 2359296 | tf_op jit(solution)/shard_map/all_gather | solution.py:56
  32.3 661.1 %reduce-scatter.2.cloned.1.call-start = ((), (), s32[]{:S(2)}) async-start(), calls=%async_computation.5 | async-start | bytes 4259840 | tf_op jit(solution)/shard_map/reduce_scatter | solution.py:100
  372.6 20.9 %collective-permute-start = (bf16[127,128]{0,1:T(8,128)(2,1)S(1)}, bf16[127,128]{0,1:T(8,128)(2,1)S(1)}, u32[]{:S(2)}, u32[]{:S(2)}) collective-permute-start(bf16[127,128]{0,1:T(8,128)(2,1)S(1)} %slice.49), channel_id=1, source_target_pairs={{0,64},{64,128},{128,192},{192,256},{256,320},{320,384},{384,448},... | collective-permute-start | bytes 97544 | tf_op jit(solution)/shard_map/ppermute | solution.py:12
  376.0 13.8 %copy-start.1 = (f32[8,128]{1,0:T(8,128)S(1)}, f32[8,128]{1,0:T(8,128)}, u32[]{:S(2)}) copy-start(f32[8,128]{1,0:T(8,128)} %param.13) | copy-start | bytes 12292
  390.0 37.0 %collective-permute-start.1 = (bf16[127,128]{0,1:T(8,128)(2,1)S(1)}, bf16[127,128]{0,1:T(8,128)(2,1)S(1)}, u32[]{:S(2)}, u32[]{:S(2)}) collective-permute-start(bf16[127,128]{0,1:T(8,128)(2,1)S(1)} %slice.48), channel_id=1, source_target_pairs={{64,0},{128,64},{192,128},{256,192},{320,256},{384,320},{448,384},... | collective-permute-start | bytes 97544 | tf_op jit(solution)/shard_map/ppermute | solution.py:12
Sparse Core Ops, SparseCore 0:
  10.1 164.2 all-gather.3
  177.4 138.5 all-gather.7
  318.1 52.1 all-gather.5
  470.3 223.0 reduce-scatter.1
